TPU v7x, 32 devices: a whole 2x2x4 slice. The times are simulated.
32 devices in a mesh: dp: 16 (over z, y, x), tensor: 2 (over core).
Axes of the slice: x: 2, y: 2, z: 4, core: 2. Of those that a mesh axis runs over, the one named last changes fastest.
Arguments:
- inputs: bfloat16 [25088, 512], P(('dp', 'tensor')), may hold values from -6 to 6
- cotangent: bfloat16 [25088, 512], P(('dp', 'tensor')), may hold values from -6 to 6
- region_ids: int32 [196], replicated, may hold values from 0 to 3
- rel_index: int32 [49, 49], replicated, may hold values from 0 to 168
- norm1_gain: bfloat16 [2, 512], replicated, may hold values from 0.5 to 1.5
- norm1_bias: bfloat16 [2, 512], replicated, may hold values from -1.75 to 1.75
- w_qkv: bfloat16 [2, 3, 512, 512], P(None, None, 'dp', 'tensor'), may hold values from -0.25 to 0.25
- qv_bias: bfloat16 [2, 2, 512], P(None, None, 'tensor'), may hold values from -1.75 to 1.75
- bias_table: bfloat16 [2, 16, 169], P(None, 'tensor'), may hold values from -3 to 250
- w_proj: bfloat16 [2, 512, 512], P(None, 'tensor', 'dp'), may hold values from -0.75 to 0.75
- proj_bias: bfloat16 [2, 512], replicated, may hold values from -1.75 to 1.75
- norm2_gain: bfloat16 [2, 512], replicated, may hold values from 0.5 to 1.5
- norm2_bias: bfloat16 [2, 512], replicated, may hold values from -1.75 to 1.75
- w_fc1: bfloat16 [2, 512, 2048], P(None, 'dp', 'tensor'), may hold values from -0.25 to 0.25
- fc1_bias: bfloat16 [2, 2048], P(None, 'tensor'), may hold values from -3 to 3
- w_fc2: bfloat16 [2, 2048, 512], P(None, 'tensor', 'dp'), may hold values from -0.125 to 0.125
- fc2_bias: bfloat16 [2, 512], replicated, may hold values from -1.75 to 1.75
Outputs:
- outputs: float32 [25088, 512], P(('dp', 'tensor'))
- input_grad: float32 [25088, 512], P(('dp', 'tensor'))
- norm1_gain_grad: float32 [2, 512], replicated
- norm1_bias_grad: float32 [2, 512], replicated
- w_qkv_grad: float32 [2, 3, 512, 512], P(None, None, 'dp', 'tensor')
- qv_bias_grad: float32 [2, 2, 512], P(None, None, 'tensor')
- bias_table_grad: float32 [2, 16, 169], P(None, 'tensor')
- w_proj_grad: float32 [2, 512, 512], P(None, 'tensor', 'dp')
- proj_bias_grad: float32 [2, 512], replicated
- norm2_gain_grad: float32 [2, 512], replicated
- norm2_bias_grad: float32 [2, 512], replicated
- w_fc1_grad: float32 [2, 512, 2048], P(None, 'dp', 'tensor')
- fc1_bias_grad: float32 [2, 2048], P(None, 'tensor')
- w_fc2_grad: float32 [2, 2048, 512], P(None, 'tensor', 'dp')
- fc2_bias_grad: float32 [2, 512], replicated
All inputs are finite; a program needn't handle non-finite values.
Results may differ from a plain program's by a relative error of at most 0.025.
Values may be sent and summed in bfloat16 or wider, within the bound.
A program may use at most 192 MiB of HBM per device.

v0:
```python
import jax
import jax.numpy as jnp
from jax import lax
from jax.sharding import PartitionSpec as P

HD = 32
GRID = 14
WIN = 7
SHIFT = 3
LAYERS = 2
TABLE = 169
EPS = 1e-05
MASKED = -100.0
EXACT_PRECISION = lax.Precision.HIGHEST


def to_grid(tokens, images):
    per_side = GRID // WIN
    shaped = tokens.reshape(images, per_side, per_side, WIN, WIN, -1)
    return shaped.transpose(0, 1, 3, 2, 4, 5).reshape(images, GRID, GRID, -1)


def to_windows(grid_rows, images):
    per_side = GRID // WIN
    shaped = grid_rows.reshape(images, per_side, WIN, per_side, WIN, -1)
    return shaped.transpose(0, 1, 3, 2, 4, 5).reshape(images * GRID * GRID, -1)


def rolled(tokens, images, offset):
    return to_windows(jnp.roll(to_grid(tokens, images), offset, axis=(1, 2)), images)


def normalize(residual):
    average = jnp.mean(residual, -1, keepdims=True)
    centered = residual - average
    inverse = lax.rsqrt(jnp.mean(centered * centered, -1, keepdims=True) + EPS)
    return (centered * inverse, inverse)


def norm_back(grad_out, normed, inverse, gain_value):
    scaled = grad_out * gain_value
    return inverse * (
        scaled
        - jnp.mean(scaled, -1, keepdims=True)
        - normed * jnp.mean(scaled * normed, -1, keepdims=True)
    )


def gelu_parts(hidden_pre):
    cumulative = 0.5 * (1.0 + lax.erf(hidden_pre * 0.7071067811865476))
    density = jnp.exp(-0.5 * hidden_pre * hidden_pre) * 0.3989422804014327
    return (hidden_pre * cumulative, cumulative + hidden_pre * density)


def product(first_operand, second_operand):
    return jnp.dot(first_operand, second_operand, preferred_element_type=jnp.float32)


def mixed_einsum(pattern, first_operand, second_operand):
    return jnp.einsum(pattern, first_operand, second_operand, preferred_element_type=jnp.float32)


def exact_einsum(pattern, first_operand, second_operand):
    return jnp.einsum(pattern, first_operand, second_operand, precision=EXACT_PRECISION)


def per_device(
    inputs,
    cotangent,
    region_ids,
    rel_index,
    norm1_gain,
    norm1_bias,
    w_qkv,
    qv_bias,
    bias_table,
    w_proj,
    proj_bias,
    norm2_gain,
    norm2_bias,
    w_fc1,
    fc1_bias,
    w_fc2,
    fc2_bias,
):
    groups = lax.axis_size("tensor")
    gathered_rows = inputs.shape[0] * groups
    images = gathered_rows // (GRID * GRID)
    heads_local = bias_table.shape[1]
    width_local = heads_local * HD
    per_side = GRID // WIN
    windows = per_side * per_side
    win_tokens = WIN * WIN
    score_scale = HD ** (-0.5)
    head_shape = (images, windows, win_tokens, heads_local, HD)
    one_hot = (rel_index[:, :, None] == jnp.arange(TABLE, dtype=jnp.int32)[None, None, :]).astype(
        jnp.float32
    )
    regions = region_ids.reshape(windows, win_tokens)
    shift_mask = jnp.where(regions[:, :, None] == regions[:, None, :], 0.0, MASKED).astype(
        jnp.float32
    )
    mask_list = [jnp.zeros_like(shift_mask), shift_mask]
    rel_biases = [
        exact_einsum("ijm,hm->hij", one_hot, bias_table[layer_index].astype(jnp.float32))
        for layer_index in range(LAYERS)
    ]

    def scores_of(layer_index, queries, key_rows):
        return (
            mixed_einsum("bwihd,bwjhd->bwhij", queries, key_rows)
            + rel_biases[layer_index][None, None]
            + mask_list[layer_index % 2][None, :, None]
        )

    def layer_backward(layer_index, stored, grad_out):
        shifted_layer = layer_index % 2 == 1
        (
            normed_attn,
            inverse_attn,
            attn_in,
            queries,
            key_rows,
            values,
            log_total,
            mixture,
            normed_ffn,
            inverse_ffn,
            ffn_in,
            gelu_slope,
            hidden,
            stacked_qkv,
            proj_rows,
            fc1_cols,
            fc2_rows,
        ) = stored
        grad_fc2_bias = jnp.sum(grad_out, 0)
        grad_low = grad_out.astype(jnp.bfloat16)
        grad_rows = lax.all_gather(grad_low, "tensor", axis=0, tiled=True)
        grad_hidden = product(grad_rows, fc2_rows.T)
        grad_w_fc2 = product(hidden.T, grad_rows)
        grad_pre = grad_hidden * gelu_slope
        grad_pre_low = grad_pre.astype(jnp.bfloat16)
        grad_fc1_bias = jnp.sum(grad_pre, 0)
        grad_w_fc1 = product(ffn_in.T, grad_pre_low)
        grad_ffn_rows = product(grad_pre_low, fc1_cols.T)
        grad_ffn_in = lax.psum_scatter(
            grad_ffn_rows.astype(jnp.bfloat16), "tensor", scatter_dimension=0, tiled=True
        ).astype(jnp.float32)
        grad_norm2_gain = jnp.sum(grad_ffn_in * normed_ffn, 0)
        grad_norm2_bias = jnp.sum(grad_ffn_in, 0)
        grad_mid = grad_out + norm_back(
            grad_ffn_in, normed_ffn, inverse_ffn, norm2_gain[layer_index].astype(jnp.float32)
        )
        grad_proj_bias = jnp.sum(grad_mid, 0)
        grad_mid_rows = lax.all_gather(grad_mid.astype(jnp.bfloat16), "tensor", axis=0, tiled=True)
        if shifted_layer:
            grad_mid_rows = rolled(grad_mid_rows, images, -SHIFT)
        grad_mixture = product(grad_mid_rows, proj_rows.T)
        grad_w_proj = product(mixture.T, grad_mid_rows)
        grad_mixture_low = grad_mixture.astype(jnp.bfloat16).reshape(head_shape)
        scores = scores_of(layer_index, queries, key_rows)
        attention = jnp.exp(scores - log_total)
        attention_low = attention.astype(jnp.bfloat16)
        grad_values = mixed_einsum("bwhij,bwihd->bwjhd", attention_low, grad_mixture_low).reshape(
            gathered_rows, width_local
        )
        grad_attention = mixed_einsum("bwihd,bwjhd->bwhij", grad_mixture_low, values)
        row_inner = jnp.sum(attention * grad_attention, -1, keepdims=True)
        grad_scores = attention * (grad_attention - row_inner)
        grad_table = exact_einsum("ijm,hij->hm", one_hot, jnp.sum(grad_scores, (0, 1)))
        grad_scores_low = grad_scores.astype(jnp.bfloat16)
        grad_queries = (
            mixed_einsum("bwhij,bwjhd->bwihd", grad_scores_low, key_rows).reshape(
                gathered_rows, width_local
            )
            * score_scale
        )
        grad_keys = mixed_einsum("bwhij,bwihd->bwjhd", grad_scores_low, queries).reshape(
            gathered_rows, width_local
        )
        grad_qv_bias = jnp.stack([jnp.sum(grad_queries, 0), jnp.sum(grad_values, 0)])
        grad_parts = [
            grad_queries.astype(jnp.bfloat16),
            grad_keys.astype(jnp.bfloat16),
            grad_values.astype(jnp.bfloat16),
        ]
        grad_attn_rows = (
            product(grad_parts[0], stacked_qkv[0].T)
            + product(grad_parts[1], stacked_qkv[1].T)
            + product(grad_parts[2], stacked_qkv[2].T)
        )
        grad_w_qkv = jnp.stack([product(attn_in.T, grad_part) for grad_part in grad_parts])
        if shifted_layer:
            grad_attn_rows = rolled(grad_attn_rows, images, SHIFT)
        grad_attn_in = lax.psum_scatter(
            grad_attn_rows.astype(jnp.bfloat16), "tensor", scatter_dimension=0, tiled=True
        ).astype(jnp.float32)
        grad_norm1_gain = jnp.sum(grad_attn_in * normed_attn, 0)
        grad_norm1_bias = jnp.sum(grad_attn_in, 0)
        grad_in = grad_mid + norm_back(
            grad_attn_in, normed_attn, inverse_attn, norm1_gain[layer_index].astype(jnp.float32)
        )
        grad_w_qkv, grad_w_proj, grad_w_fc1, grad_w_fc2 = (
            lax.psum_scatter(
                grad_w_qkv.astype(jnp.bfloat16), "dp", scatter_dimension=1, tiled=True
            ).astype(jnp.float32),
            lax.psum_scatter(
                grad_w_proj.astype(jnp.bfloat16), "dp", scatter_dimension=1, tiled=True
            ).astype(jnp.float32),
            lax.psum_scatter(
                grad_w_fc1.astype(jnp.bfloat16), "dp", scatter_dimension=0, tiled=True
            ).astype(jnp.float32),
            lax.psum_scatter(
                grad_w_fc2.astype(jnp.bfloat16), "dp", scatter_dimension=1, tiled=True
            ).astype(jnp.float32),
        )
        return (
            grad_in,
            (
                grad_norm1_gain,
                grad_norm1_bias,
                grad_w_qkv,
                grad_qv_bias,
                grad_table,
                grad_w_proj,
                grad_proj_bias,
                grad_norm2_gain,
                grad_norm2_bias,
                grad_w_fc1,
                grad_fc1_bias,
                grad_w_fc2,
                grad_fc2_bias,
            ),
        )

    residual = inputs.astype(jnp.float32)
    forward_store = []
    for layer_index in range(LAYERS):
        layer_shifted_layer = layer_index % 2 == 1
        layer_stacked_qkv = lax.all_gather(w_qkv[layer_index], "dp", axis=1, tiled=True)
        layer_proj_rows = lax.all_gather(w_proj[layer_index], "dp", axis=1, tiled=True)
        layer_fc1_cols = lax.all_gather(w_fc1[layer_index], "dp", axis=0, tiled=True)
        layer_fc2_rows = lax.all_gather(w_fc2[layer_index], "dp", axis=1, tiled=True)
        up_bias = fc1_bias[layer_index]
        layer_normed_attn, layer_inverse_attn = normalize(residual)
        attn_local = (
            layer_normed_attn * norm1_gain[layer_index].astype(jnp.float32)
            + norm1_bias[layer_index].astype(jnp.float32)
        ).astype(jnp.bfloat16)
        layer_attn_in = lax.all_gather(attn_local, "tensor", axis=0, tiled=True)
        if layer_shifted_layer:
            layer_attn_in = rolled(layer_attn_in, images, -SHIFT)
        query_pre = product(layer_attn_in, layer_stacked_qkv[0]) + qv_bias[layer_index, 0].astype(
            jnp.float32
        )
        layer_queries = (query_pre * score_scale).astype(jnp.bfloat16).reshape(head_shape)
        layer_key_rows = (
            product(layer_attn_in, layer_stacked_qkv[1]).astype(jnp.bfloat16).reshape(head_shape)
        )
        layer_values = (
            (
                product(layer_attn_in, layer_stacked_qkv[2])
                + qv_bias[layer_index, 1].astype(jnp.float32)
            )
            .astype(jnp.bfloat16)
            .reshape(head_shape)
        )
        layer_scores = scores_of(layer_index, layer_queries, layer_key_rows)
        highest = jnp.max(layer_scores, -1, keepdims=True)
        exponent = jnp.exp(layer_scores - highest)
        denominator = jnp.sum(exponent, -1, keepdims=True)
        layer_attention = exponent / denominator
        layer_log_total = highest + jnp.log(denominator)
        layer_mixture = (
            mixed_einsum("bwhij,bwjhd->bwihd", layer_attention.astype(jnp.bfloat16), layer_values)
            .astype(jnp.bfloat16)
            .reshape(gathered_rows, width_local)
        )
        projected = product(layer_mixture, layer_proj_rows)
        if layer_shifted_layer:
            projected = rolled(projected, images, SHIFT)
        residual_mid = (
            residual
            + lax.psum_scatter(
                projected.astype(jnp.bfloat16), "tensor", scatter_dimension=0, tiled=True
            ).astype(jnp.float32)
            + proj_bias[layer_index].astype(jnp.float32)
        )
        layer_normed_ffn, layer_inverse_ffn = normalize(residual_mid)
        ffn_local = (
            layer_normed_ffn * norm2_gain[layer_index].astype(jnp.float32)
            + norm2_bias[layer_index].astype(jnp.float32)
        ).astype(jnp.bfloat16)
        layer_ffn_in = lax.all_gather(ffn_local, "tensor", axis=0, tiled=True)
        hidden_pre = product(layer_ffn_in, layer_fc1_cols) + up_bias.astype(jnp.float32)
        activated, layer_gelu_slope = gelu_parts(hidden_pre)
        layer_hidden = activated.astype(jnp.bfloat16)
        down_part = product(layer_hidden, layer_fc2_rows)
        down_sum = lax.psum_scatter(
            down_part.astype(jnp.bfloat16), "tensor", scatter_dimension=0, tiled=True
        ).astype(jnp.float32)
        residual_out = residual_mid + down_sum + fc2_bias[layer_index].astype(jnp.float32)
        layer_stored = (
            layer_normed_attn,
            layer_inverse_attn,
            layer_attn_in,
            layer_queries,
            layer_key_rows,
            layer_values,
            layer_log_total,
            layer_mixture,
            layer_normed_ffn,
            layer_inverse_ffn,
            layer_ffn_in,
            layer_gelu_slope,
            layer_hidden,
            layer_stacked_qkv,
            layer_proj_rows,
            layer_fc1_cols,
            layer_fc2_rows,
        )
        residual = residual_out
        stored = layer_stored
        forward_store.append(stored)
    grad_residual = cotangent.astype(jnp.float32)
    layer_grads = [None] * LAYERS
    for layer_index in reversed(range(LAYERS)):
        grad_residual, layer_grads[layer_index] = layer_backward(
            layer_index, forward_store[layer_index], grad_residual
        )
    stacked = [
        jnp.stack([layer_grads[layer_index][position] for layer_index in range(LAYERS)])
        for position in range(13)
    ]
    qv_total, fc1_total, table_total = lax.psum((stacked[3], stacked[10], stacked[4]), "dp")
    gain1_total, bias1_total, proj_total, gain2_total, bias2_total, fc2_total = lax.psum(
        (stacked[0], stacked[1], stacked[6], stacked[7], stacked[8], stacked[12]), ("dp", "tensor")
    )
    return (
        residual,
        grad_residual,
        gain1_total,
        bias1_total,
        stacked[2],
        qv_total,
        table_total,
        stacked[5],
        proj_total,
        gain2_total,
        bias2_total,
        stacked[9],
        fc1_total,
        stacked[11],
        fc2_total,
    )


def solution(mesh):
    in_specs = (
        P(("dp", "tensor"), None),
        P(("dp", "tensor"), None),
        P(),
        P(),
        P(),
        P(),
        P(None, None, "dp", "tensor"),
        P(None, None, "tensor"),
        P(None, "tensor", None),
        P(None, "tensor", "dp"),
        P(),
        P(),
        P(),
        P(None, "dp", "tensor"),
        P(None, "tensor"),
        P(None, "tensor", "dp"),
        P(),
    )
    out_specs = (
        P(("dp", "tensor"), None),
        P(("dp", "tensor"), None),
        P(),
        P(),
        P(None, None, "dp", "tensor"),
        P(None, None, "tensor"),
        P(None, "tensor", None),
        P(None, "tensor", "dp"),
        P(),
        P(),
        P(),
        P(None, "dp", "tensor"),
        P(None, "tensor"),
        P(None, "tensor", "dp"),
        P(),
    )
    return jax.shard_map(
        per_device, mesh=mesh, in_specs=in_specs, out_specs=out_specs, check_vma=False
    )
```

profile of v0, /device:TPU:0, one launch (start us, length us, event | category | flops | bytes accessed | tf_op | source)
XLA Modules:
  0.0 1455.0 jit_solution(11399592159413549358)
XLA Ops:
  14.0 44.0 %all-gather.1 = bf16[1,256,512]{1,2,0:T(8,128)(2,1)S(1)} all-gather(bf16[1,256,32]{1,2,0:T(8,128)(2,1)S(1)} %get-tuple-element.65), channel_id=3, replica_groups=mesh['dp'=16,'tensor'=2] {'dp'}, dimensions={2}, use_global_device_ids=true | all-gather | bytes 278528 | tf_op jit(solution)/shard_map/all_gather | solution.py:242
  58.1 40.2 %all-gather = bf16[1,3,512,256]{3,2,1,0:T(8,128)(2,1)S(1)} all-gather(bf16[1,3,32,256]{3,2,1,0:T(8,128)(2,1)S(1)} %get-tuple-element.63), channel_id=2, replica_groups=mesh['dp'=16,'tensor'=2] {'dp'}, dimensions={2}, use_global_device_ids=true | all-gather | bytes 835584 | tf_op jit(solution)/shard_map/all_gather | solution.py:241
  127.6 5.5 copy.116
  153.0 6.3 reduce-scatter.17.cloned.1.call-done
  163.7 45.4 %all-gather.37.cloned.1.call-done = bf16[1,512,1024]{2,1,0:T(8,128)(2,1)} async-done(((bf16[1,32,1024]{2,1,0:T(8,128)(2,1)}), bf16[1,512,1024]{2,1,0:T(8,128)(2,1)}) %all-gather.37.cloned.1.call-update) | async-done | bytes 1048592 | tf_op jit(solution)/shard_map/all_gather | solution.py:243
  209.1 10.6 all-gather.23.cloned.1.call-done
  219.7 6.2 multiply_convert_fusion.1
  225.9 53.4 %all-gather.39.cloned.1.call-done = bf16[1,1024,512]{1,2,0:T(8,128)(2,1)} async-done(((bf16[1,1024,32]{1,2,0:T(8,128)(2,1)}), bf16[1,1024,512]{1,2,0:T(8,128)(2,1)}) %all-gather.39.cloned.1.call-update) | async-done | bytes 1048592 | tf_op jit(solution)/shard_map/all_gather | solution.py:244
  279.3 5.2 convolution_convert_fusion.3
  285.2 7.5 reduce-scatter.19.cloned.1.call-done
  297.1 42.3 %all-gather.5 = bf16[1,256,512]{1,2,0:T(8,128)(2,1)S(1)} all-gather(bf16[1,256,32]{1,2,0:T(8,128)(2,1)S(1)} %get-tuple-element.64), channel_id=7, replica_groups=mesh['dp'=16,'tensor'=2] {'dp'}, dimensions={2}, use_global_device_ids=true | all-gather | bytes 278528 | tf_op jit(solution)/shard_map/all_gather | solution.py:242
  339.5 40.2 %all-gather.4 = bf16[1,3,512,256]{3,2,1,0:T(8,128)(2,1)S(1)} all-gather(bf16[1,3,32,256]{3,2,1,0:T(8,128)(2,1)S(1)} %get-tuple-element.62), channel_id=6, replica_groups=mesh['dp'=16,'tensor'=2] {'dp'}, dimensions={2}, use_global_device_ids=true | all-gather | bytes 835584 | tf_op jit(solution)/shard_map/all_gather | solution.py:241
  402.8 4.9 copy.128
  417.7 5.1 copy.127
  433.3 7.2 copy.132
  452.3 6.2 reduce-scatter.21.cloned.1.call-done
  463.5 54.9 %all-gather.41.cloned.1.call-done = bf16[1,512,1024]{2,1,0:T(8,128)(2,1)} async-done(((bf16[1,32,1024]{2,1,0:T(8,128)(2,1)}), bf16[1,512,1024]{2,1,0:T(8,128)(2,1)}) %all-gather.41.cloned.1.call-update) | async-done | bytes 1048592 | tf_op jit(solution)/shard_map/all_gather | solution.py:243
  518.4 10.6 all-gather.27.cloned.1.call-done
  529.0 6.9 multiply_convert_fusion
  535.9 5.4 all-gather.29.cloned.1.call-done
  541.4 59.0 %all-gather.43.cloned.1.call-done = bf16[1,1024,512]{1,2,0:T(8,128)(2,1)} async-done(((bf16[1,1024,32]{1,2,0:T(8,128)(2,1)}), bf16[1,1024,512]{1,2,0:T(8,128)(2,1)}) %all-gather.43.cloned.1.call-update) | async-done | bytes 1048592 | tf_op jit(solution)/shard_map/all_gather | solution.py:244
  600.4 7.0 fusion.147
  613.3 5.0 convolution_convert_fusion.2
  622.3 10.4 reduce-scatter.23.cloned.1.call-done
  638.7 10.5 all-gather.31.cloned.1.call-done
  658.7 5.1 copy.139
  663.8 6.9 multiply_reduce_fusion.1
  696.0 5.0 convert_element_type.366
  716.6 10.4 reduce-scatter.27.cloned.1.call-done
  732.0 11.1 all-gather.33.cloned.1.call-done
  743.0 6.4 fusion.148
  754.4 10.1 reduce-scatter.29.cloned.1.call-done
  770.8 5.0 convolution_convert_fusion.9
  775.9 5.9 convolution_convert_fusion.10
  781.8 5.1 fusion.90
  787.1 5.0 fusion.93
  818.2 4.9 copy.153
  823.2 7.3 multiply_reduce_fusion
  851.4 5.2 convert_element_type.385
  894.3 38.9 %reduce-scatter.45.cloned.1.call-done = bf16[1024,32]{0,1:T(8,128)(2,1)} async-done(((bf16[1024,512]{0,1:T(8,128)(2,1)}), bf16[1024,32]{0,1:T(8,128)(2,1)}) %reduce-scatter.45.cloned.1.call-update) | async-done | bytes 65552 | tf_op jit(solution)/shard_map/reduce_scatter | solution.py:214
  934.8 75.7 %reduce-scatter.43.cloned.1.call-done = bf16[32,1024]{1,0:T(8,128)(2,1)} async-done(((bf16[512,1024]{1,0:T(8,128)(2,1)}), bf16[32,1024]{1,0:T(8,128)(2,1)}) %reduce-scatter.43.cloned.1.call-update) | async-done | bytes 65552 | tf_op jit(solution)/shard_map/reduce_scatter | solution.py:211
  1010.5 77.4 %reduce-scatter.41.cloned.1.call-done = bf16[32,1024]{1,0:T(8,128)(2,1)} async-done(((bf16[512,1024]{1,0:T(8,128)(2,1)}), bf16[32,1024]{1,0:T(8,128)(2,1)}) %reduce-scatter.41.cloned.1.call-update) | async-done | bytes 65552 | tf_op jit(solution)/shard_map/reduce_scatter | solution.py:211
  1093.7 72.7 %all-reduce.1 = (f32[2,2,256]{2,1,0:T(2,128)}, f32[2,8,169]{2,1,0:T(8,128)}, f32[2,1024]{1,0:T(2,128)}) all-reduce(f32[2,2,256]{2,1,0:T(2,128)S(1)} %pad_maximum_fusion.12, f32[2,8,169]{2,1,0:T(8,128)S(1)} %pad_maximum_fusion.8, f32[2,1024]{1,0:T(2,128)S(1)} %pad_maximum_fusion.9), channel_id=1, replica_groups=mesh['dp'=16,'tensor'=2] {'dp'}, use_global_device_ids=true, to_apply=%region_42.43 | all-reduce | flops 5776 | bytes 46208 | tf_op jit(solution)/shard_map/psum | solution.py:336
  1166.4 73.0 %reduce-scatter.37.cloned.1.call-done = bf16[256,32]{0,1:T(8,128)(2,1)} async-done(((bf16[256,512]{0,1:T(8,128)(2,1)}), bf16[256,32]{0,1:T(8,128)(2,1)}) %reduce-scatter.37.cloned.1.call-update) | async-done | bytes 16400 | tf_op jit(solution)/shard_map/reduce_scatter | solution.py:208
  1240.8 75.4 %reduce-scatter.35.cloned.1.call-done = bf16[3,32,256]{2,1,0:T(8,128)(2,1)} async-done(((bf16[3,512,256]{2,1,0:T(8,128)(2,1)}), bf16[3,32,256]{2,1,0:T(8,128)(2,1)}) %reduce-scatter.35.cloned.1.call-update) | async-done | bytes 49168 | tf_op jit(solution)/shard_map/reduce_scatter | solution.py:205
  1316.2 76.6 %reduce-scatter.33.cloned.1.call-done = bf16[3,32,256]{2,1,0:T(8,128)(2,1)} async-done(((bf16[3,512,256]{2,1,0:T(8,128)(2,1)}), bf16[3,32,256]{2,1,0:T(8,128)(2,1)}) %reduce-scatter.33.cloned.1.call-update) | async-done | bytes 49168 | tf_op jit(solution)/shard_map/reduce_scatter | solution.py:205
  1394.3 6.7 reduce-scatter.31.cloned.1.call-done
  1403.1 41.3 %all-reduce = (f32[2,512]{1,0:T(2,128)}, f32[2,512]{1,0:T(2,128)}, f32[2,512]{1,0:T(2,128)}, f32[2,512]{1,0:T(2,128)}, f32[2,512]{1,0:T(2,128)}, /*index=5*/f32[2,512]{1,0:T(2,128)}) all-reduce(f32[2,512]{1,0:T(2,128)S(1)} %pad_maximum_fusion.10, ...), channel_id=1, replica_groups=mesh['dp'=16,'tensor'=2] {'dp','tensor'}, use_global_device_ids=true, to_apply=%region_32.33 | all-reduce | flops 6144 | bytes 49152 | tf_op jit(solution)/shard_map/psum | solution.py:337
  (468 shorter events, 306.3 us)
Async XLA Ops:
  8.0 90.2 %all-gather.21.cloned.1.call-start = ((), (), s32[]{:S(2)}) async-start(), calls=%async_computation.16 | async-start | bytes 2408448 | tf_op jit(solution)/shard_map/all_gather | solution.py:251
  13.0 45.1 %copy-start.83 = (bf16[2,2,256]{2,1,0:T(2,128)(2,1)S(1)}, bf16[2,2,256]{2,1,0:T(2,128)(2,1)}, u32[]{:S(2)}) copy-start(bf16[2,2,256]{2,1,0:T(2,128)(2,1)} %param.24) | copy-start | bytes 6148
  13.0 45.1 %copy-start.70 = (bf16[2,3,32,256]{3,2,1,0:T(8,128)(2,1)S(1)}, bf16[2,3,32,256]{3,2,1,0:T(8,128)(2,1)}, u32[]{:S(2)}) copy-start(bf16[2,3,32,256]{3,2,1,0:T(8,128)(2,1)} %param.23) | copy-start | bytes 294916
  13.0 146.4 %reduce-scatter.17.cloned.1.call-start = ((), (), s32[]{:S(2)}) async-start(), calls=%async_computation.17 | async-start | bytes 2408448 | tf_op jit(solution)/shard_map/reduce_scatter | solution.py:285
  14.0 125.1 %copy-start.28 = (f32[8,49,49]{1,2,0:T(8,128)}, f32[8,49,49]{1,2,0:T(8,128)S(1)}, u32[]{:S(2)}) copy-start(f32[8,49,49]{1,2,0:T(8,128)S(1)} %copy.118) | copy-start | bytes 230500
  58.0 91.0 %copy-start.47 = (bf16[1,256,512]{1,2,0:T(8,128)(2,1)}, bf16[1,256,512]{1,2,0:T(8,128)(2,1)S(1)}, u32[]{:S(2)}) copy-start(bf16[1,256,512]{1,2,0:T(8,128)(2,1)S(1)} %all-gather.1) | copy-start | bytes 786436
  106.9 26.1 %copy-start.13 = (bf16[8,4,49,8,32]{2,4,3,1,0:T(8,128)(2,1)}, bf16[8,4,49,8,32]{2,4,3,1,0:T(8,128)(2,1)S(1)}, u32[]{:S(2)}) copy-start(bf16[8,4,49,8,32]{2,4,3,1,0:T(8,128)(2,1)S(1)} %copy.117) | copy-start | bytes 2408452
  152.0 57.1 %all-gather.37.cloned.1.call-start = ((), (), s32[]{:S(2)}) async-start(), calls=%async_computation.40 | async-start | bytes 1114112 | tf_op jit(solution)/shard_map/all_gather | solution.py:243
  152.7 67.0 %all-gather.23.cloned.1.call-start = ((), (), s32[]{:S(2)}) async-start(), calls=%async_computation.18 | async-start | bytes 2408448 | tf_op jit(solution)/shard_map/all_gather | solution.py:295
  162.9 116.4 %all-gather.39.cloned.1.call-start = ((), (), s32[]{:S(2)}) async-start(), calls=%async_computation.41 | async-start | bytes 1114112 | tf_op jit(solution)/shard_map/all_gather | solution.py:244
  163.7 129.0 %reduce-scatter.19.cloned.1.call-start = ((), (), s32[]{:S(2)}) async-start(), calls=%async_computation.19 | async-start | bytes 2408448 | tf_op jit(solution)/shard_map/reduce_scatter | solution.py:300
  284.6 95.2 %all-gather.25.cloned.1.call-start = ((), (), s32[]{:S(2)}) async-start(), calls=%async_computation.20 | async-start | bytes 2408448 | tf_op jit(solution)/shard_map/all_gather | solution.py:251
  294.3 164.2 %copy-start.5 = (f32[784,512]{1,0:T(8,128)}, f32[784,512]{1,0:T(8,128)S(1)}, u32[]{:S(2)}) copy-start(f32[784,512]{1,0:T(8,128)S(1)} %get-tuple-element.53) | copy-start | bytes 4816900
  296.0 162.6 %reduce-scatter.21.cloned.1.call-start = ((), (), s32[]{:S(2)}) async-start(), calls=%async_computation.21 | async-start | bytes 2408448 | tf_op jit(solution)/shard_map/reduce_scatter | solution.py:285
  339.4 105.3 %copy-start.49 = (bf16[1,256,512]{1,2,0:T(8,128)(2,1)}, bf16[1,256,512]{1,2,0:T(8,128)(2,1)S(1)}, u32[]{:S(2)}) copy-start(bf16[1,256,512]{1,2,0:T(8,128)(2,1)S(1)} %all-gather.5) | copy-start | bytes 786436
  379.7 17.0 %copy-start.45 = (bf16[1,3,512,256]{3,2,1,0:T(8,128)(2,1)}, bf16[1,3,512,256]{3,2,1,0:T(8,128)(2,1)S(1)}, u32[]{:S(2)}) copy-start(bf16[1,3,512,256]{3,2,1,0:T(8,128)(2,1)S(1)} %all-gather.4) | copy-start | bytes 2359300
  451.5 66.8 %all-gather.41.cloned.1.call-start = ((), (), s32[]{:S(2)}) async-start(), calls=%async_computation.42 | async-start | bytes 1114112 | tf_op jit(solution)/shard_map/all_gather | solution.py:243
  452.3 76.7 %all-gather.27.cloned.1.call-start = ((), (), s32[]{:S(2)}) async-start(), calls=%async_computation.22 | async-start | bytes 2408448 | tf_op jit(solution)/shard_map/all_gather | solution.py:295
  462.3 79.1 %all-gather.29.cloned.1.call-start = ((), (), s32[]{:S(2)}) async-start(), calls=%async_computation.24 | async-start | bytes 2408448 | tf_op jit(solution)/shard_map/all_gather | solution.py:139
  462.9 137.5 %all-gather.43.cloned.1.call-start = ((), (), s32[]{:S(2)}) async-start(), calls=%async_computation.43 | async-start | bytes 1114112 | tf_op jit(solution)/shard_map/all_gather | solution.py:244
  463.5 156.7 %reduce-scatter.25.cloned.1.call-start = ((), (), s32[]{:S(2)}) async-start(), calls=%async_computation.25 | async-start | bytes 2408448 | tf_op jit(solution)/shard_map/reduce_scatter | solution.py:147
  612.1 20.6 %reduce-scatter.23.cloned.1.call-start = ((), (), s32[]{:S(2)}) async-start(), calls=%async_computation.23 | async-start | bytes 2408448 | tf_op jit(solution)/shard_map/reduce_scatter | solution.py:300
  618.3 14.4 copy-start.40
  618.3 30.9 %all-gather.31.cloned.1.call-start = ((), (), s32[]{:S(2)}) async-start(), calls=%async_computation.26 | async-start | bytes 2408448 | tf_op jit(solution)/shard_map/all_gather | solution.py:156
  637.9 89.1 %reduce-scatter.27.cloned.1.call-start = ((), (), s32[]{:S(2)}) async-start(), calls=%async_computation.27 | async-start | bytes 2408448 | tf_op jit(solution)/shard_map/reduce_scatter | solution.py:196
  691.1 19.5 %copy-start.31 = (bf16[1568,256]{0,1:T(8,128)(2,1)}, bf16[1568,256]{0,1:T(8,128)(2,1)S(1)}, u32[]{:S(2)}) copy-start(bf16[1568,256]{0,1:T(8,128)(2,1)S(1)} %convert_element_type.363) | copy-start | bytes 2408452
  716.6 26.5 %all-gather.33.cloned.1.call-start = ((), (), s32[]{:S(2)}) async-start(), calls=%async_computation.28 | async-start | bytes 2408448 | tf_op jit(solution)/shard_map/all_gather | solution.py:139
  731.9 32.6 %reduce-scatter.29.cloned.1.call-start = ((), (), s32[]{:S(2)}) async-start(), calls=%async_computation.29 | async-start | bytes 2408448 | tf_op jit(solution)/shard_map/reduce_scatter | solution.py:147
  751.1 13.4 copy-start.69
  751.1 13.4 copy-start.74
  754.2 12.7 copy-start.24
  754.2 50.9 %all-gather.35.cloned.1.call-start = ((), (), s32[]{:S(2)}) async-start(), calls=%async_computation.30 | async-start | bytes 2408448 | tf_op jit(solution)/shard_map/all_gather | solution.py:156
  770.1 124.2 %reduce-scatter.47.cloned.1.call-start = ((), (), s32[]{:S(2)}) async-start(), calls=%async_computation.39 | async-start | bytes 1114112 | tf_op jit(solution)/shard_map/reduce_scatter | solution.py:214
  775.8 157.4 %reduce-scatter.45.cloned.1.call-start = ((), (), s32[]{:S(2)}) async-start(), calls=%async_computation.38 | async-start | bytes 1114112 | tf_op jit(solution)/shard_map/reduce_scatter | solution.py:214
  781.8 228.8 %reduce-scatter.43.cloned.1.call-start = ((), (), s32[]{:S(2)}) async-start(), calls=%async_computation.37 | async-start | bytes 1114112 | tf_op jit(solution)/shard_map/reduce_scatter | solution.py:211
  787.0 300.9 %reduce-scatter.41.cloned.1.call-start = ((), (), s32[]{:S(2)}) async-start(), calls=%async_computation.36 | async-start | bytes 1114112 | tf_op jit(solution)/shard_map/reduce_scatter | solution.py:211
  792.1 374.3 %reduce-scatter.39.cloned.1.call-start = ((), (), s32[]{:S(2)}) async-start(), calls=%async_computation.35 | async-start | bytes 278528 | tf_op jit(solution)/shard_map/reduce_scatter | solution.py:208
  803.6 435.8 %reduce-scatter.37.cloned.1.call-start = ((), (), s32[]{:S(2)}) async-start(), calls=%async_computation.34 | async-start | bytes 278528 | tf_op jit(solution)/shard_map/reduce_scatter | solution.py:208
  808.1 508.1 %reduce-scatter.35.cloned.1.call-start = ((), (), s32[]{:S(2)}) async-start(), calls=%async_computation.33 | async-start | bytes 835584 | tf_op jit(solution)/shard_map/reduce_scatter | solution.py:205
  811.2 581.5 %reduce-scatter.33.cloned.1.call-start = ((), (), s32[]{:S(2)}) async-start(), calls=%async_computation.32 | async-start | bytes 835584 | tf_op jit(solution)/shard_map/reduce_scatter | solution.py:205
  813.5 17.0 %slice-start = ((s8[7340032]{0:T(1024)(128)(4,1)}), s8[3145728]{0:T(1024)(128)(4,1)S(1)}, s32[]{:S(2)}) async-start(s8[7340032]{0:T(1024)(128)(4,1)} %bitcast.277), calls=%async_computation.44 | async-start | bytes 6291456
  873.8 527.2 %reduce-scatter.31.cloned.1.call-start = ((), (), s32[]{:S(2)}) async-start(), calls=%async_computation.31 | async-start | bytes 2408448 | tf_op jit(solution)/shard_map/reduce_scatter | solution.py:196
  893.1 196.4 %copy-start.57 = (f32[8,49,49]{1,2,0:T(8,128)S(1)}, f32[8,49,49]{1,2,0:T(8,128)}, u32[]{:S(2)}) copy-start(f32[8,49,49]{1,2,0:T(8,128)} %get-tuple-element.40) | copy-start | bytes 230500
  1089.8 311.2 %copy-start.67 = (f32[784]{0:T(1024)S(1)}, f32[784]{0:T(1024)}, u32[]{:S(2)}) copy-start(f32[784]{0:T(1024)} %copy-done.66) | copy-start | bytes 9412
  1089.8 311.2 %copy-start.72 = (f32[784]{0:T(1024)S(1)}, f32[784]{0:T(1024)}, u32[]{:S(2)}) copy-start(f32[784]{0:T(1024)} %copy-done.71) | copy-start | bytes 9412
  1089.8 311.2 %copy-start.76 = (f32[1,512]{1,0:T(1,128)S(1)}, f32[1,512]{1,0:T(1,128)}, u32[]{:S(2)}) copy-start(f32[1,512]{1,0:T(1,128)} %copy-done.75) | copy-start | bytes 6148
  1092.5 308.5 %copy-start.4 = (bf16[784,512]{1,0:T(8,128)(2,1)S(1)}, bf16[784,512]{1,0:T(8,128)(2,1)}, u32[]{:S(2)}) copy-start(bf16[784,512]{1,0:T(8,128)(2,1)} %param.17) | copy-start | bytes 2408452
  1092.5 351.9 %copy-start.20 = (f32[784,512]{1,0:T(8,128)S(1)}, f32[784,512]{1,0:T(8,128)}, u32[]{:S(2)}) copy-start(f32[784,512]{1,0:T(8,128)} %copy-done.19) | copy-start | bytes 4816900
  (88 other events, 325.0 us)
Sparse Core Ops, SparseCore 0:
  13.1 12.5 all-gather.20
  152.1 7.1 reduce-scatter.16
  284.7 7.9 reduce-scatter.18
  612.2 7.9 reduce-scatter.24
  622.3 10.3 reduce-scatter.22
  638.0 11.1 all-gather.30
  716.7 10.2 reduce-scatter.26
  770.2 11.1 all-gather.34
Sparse Core Ops, SparseCore 1:
  155.8 53.2 all-gather.36
  211.1 8.6 all-gather.22
  222.9 56.3 all-gather.38
  296.0 11.0 all-gather.24
  451.6 6.8 reduce-scatter.20
  461.9 56.4 all-gather.40
  520.4 8.6 all-gather.26
  530.4 10.9 all-gather.28
  544.0 56.3 all-gather.42
  732.0 11.0 all-gather.32
  754.3 10.1 reduce-scatter.28
  775.9 80.0 reduce-scatter.46
  858.1 75.1 reduce-scatter.44
  935.5 75.0 reduce-scatter.42
  1012.8 75.0 reduce-scatter.40
  1090.2 73.5 reduce-scatter.38
  1166.0 73.3 reduce-scatter.36
  1241.7 74.5 reduce-scatter.34
  1318.3 74.4 reduce-scatter.32
  1395.6 5.3 reduce-scatter.30
where the time goes:
time: 1460 us
  waiting for transfers between devices  739 us (51%)
  blocking collectives  281 us (19%)
  local copies, waits for them, and re-layouts  194 us (13%)
  matrix products  157 us (11%)
  other arithmetic  64.5 us (4%)
  between operations  17.7 us (1%)
    reduce_scatter x2, waiting for transfers between devices, layer_backward(): lax.psum_scatter(grad_w_fc1.astype(jnp.bfloat16), 'dp', scatter_dimension...  153 us
    reduce_scatter x2, waiting for transfers between devices, layer_backward(): lax.psum_scatter(grad_w_qkv.astype(jnp.bfloat16), 'dp', scatter_dimension...  152 us
    all_gather x2, waiting for transfers between devices, per_device(): lax.all_gather(w_fc2[layer_index], 'dp', axis=1, tiled=True)  112 us
    dot_general x36, matrix products, product(): jnp.dot(first_operand, second_operand, preferred_element_type=jnp.float32)  106 us
    all_gather x2, waiting for transfers between devices, per_device(): lax.all_gather(w_fc1[layer_index], 'dp', axis=0, tiled=True)  100 us
    all_gather x2, blocking collectives, per_device(): lax.all_gather(w_proj[layer_index], 'dp', axis=1, tiled=True)  86.3 us
    all_gather x2, blocking collectives, per_device(): lax.all_gather(w_qkv[layer_index], 'dp', axis=1, tiled=True)  80.4 us
    reduce_scatter x2, waiting for transfers between devices, layer_backward(): lax.psum_scatter(grad_w_proj.astype(jnp.bfloat16), 'dp', scatter_dimensio...  73 us
  transfers between devices with their start and end apart: 28, of which 23 were waited for; matrix products, arithmetic and copies ran while one was open for 11% of the time, Pallas kernels for 0%

commit v1 on v0

--- a/solution.py
+++ b/solution.py
@@ -241,7 +241,15 @@
         layer_stacked_qkv = lax.all_gather(w_qkv[layer_index], "dp", axis=1, tiled=True)
         layer_proj_rows = lax.all_gather(w_proj[layer_index], "dp", axis=1, tiled=True)
         layer_fc1_cols = lax.all_gather(w_fc1[layer_index], "dp", axis=0, tiled=True)
-        layer_fc2_rows = lax.all_gather(w_fc2[layer_index], "dp", axis=1, tiled=True)
+        ways, here, step = (lax.axis_size("dp"), lax.axis_index("dp"), w_fc2[layer_index].shape[1])
+        line, have = (w_fc2[layer_index], 1)
+        while have < ways:
+            line = jnp.concatenate(
+                [line, lax.ppermute(line, "dp", [(d, (d - have) % ways) for d in range(ways)])],
+                axis=1,
+            )
+            have = 2 * have
+        layer_fc2_rows = jnp.roll(line, here * step, axis=1)
         up_bias = fc1_bias[layer_index]
         layer_normed_attn, layer_inverse_attn = normalize(residual)
         attn_local = (

time: 1460 us -> 1370 us (0.938)
  waiting for transfers between devices: 739 us -> 627 us
  starting transfers between devices: 2.17 us -> 17.8 us
    all_gather x2 -> x0, waiting for transfers between devices: 112 us -> none  [per_device(): lax.all_gather(w_fc2[layer_index], 'dp', axis=1, tiled=True)]
    all_gather x2, waiting for transfers between devices: 100 us -> 21.5 us  [per_device(): lax.all_gather(w_fc1[layer_index], 'dp', axis=0, tiled=True)]
    ppermute x0 -> x8, waiting for transfers between devices: none -> 70 us  [per_device(): lax.ppermute(line, 'dp', [(d, (d - have) % ways) for d in range(ways)])]
    ppermute x0 -> x8, starting transfers between devices: none -> 15.9 us  [per_device(): lax.ppermute(line, 'dp', [(d, (d - have) % ways) for d in range(ways)])]
  transfers between devices with their start and end apart: 28 -> 34, of which waited for: 23 -> 29; matrix products, arithmetic and copies ran while one was open for 11% -> 12% of each run, Pallas kernels for 0% -> 0%
where the time goes in v1:
time: 1370 us; the launch traced here: 1360 us
  waiting for transfers between devices  627 us (46%)
  blocking collectives  280 us (20%)
  local copies, waits for them, and re-layouts  195 us (14%)
  matrix products  157 us (11%)
  other arithmetic  68.7 us (5%)
  starting transfers between devices  17.8 us (1%)
  between operations  17.8 us (1%)
    reduce_scatter x2, waiting for transfers between devices, layer_backward(): lax.psum_scatter(grad_w_fc1.astype(jnp.bfloat16), 'dp', scatter_dimension...  153 us
    reduce_scatter x2, waiting for transfers between devices, layer_backward(): lax.psum_scatter(grad_w_qkv.astype(jnp.bfloat16), 'dp', scatter_dimension...  152 us
    dot_general x36, matrix products, product(): jnp.dot(first_operand, second_operand, preferred_element_type=jnp.float32)  106 us
    all_gather x2, blocking collectives, per_device(): lax.all_gather(w_proj[layer_index], 'dp', axis=1, tiled=True)  86.4 us
    all_gather x2, blocking collectives, per_device(): lax.all_gather(w_qkv[layer_index], 'dp', axis=1, tiled=True)  80.3 us
    reduce_scatter x2, waiting for transfers between devices, layer_backward(): lax.psum_scatter(grad_w_proj.astype(jnp.bfloat16), 'dp', scatter_dimensio...  73.2 us
    psum x1, blocking collectives, per_device(): lax.psum((stacked[3], stacked[10], stacked[4]), 'dp')  72.4 us
    ppermute x8, waiting for transfers between devices, per_device(): lax.ppermute(line, 'dp', [(d, (d - have) % ways) for d in range(ways)])  70 us
  transfers between devices with their start and end apart: 34, of which 29 were waited for; matrix products, arithmetic and copies ran while one was open for 12% of the time, Pallas kernels for 0%

profile of v1, /device:TPU:0, one launch (start us, length us, event | category | flops | bytes accessed | tf_op | source)
XLA Modules:
  0.0 1363.9 jit_solution(1751454618352343461)
XLA Ops:
  14.0 44.0 %all-gather.1 = bf16[1,256,512]{1,2,0:T(8,128)(2,1)S(1)} all-gather(bf16[1,256,32]{1,2,0:T(8,128)(2,1)S(1)} %get-tuple-element.68), channel_id=3, replica_groups=mesh['dp'=16,'tensor'=2] {'dp'}, dimensions={2}, use_global_device_ids=true | all-gather | bytes 278528 | tf_op jit(solution)/shard_map/all_gather | solution.py:242
  58.1 40.2 %all-gather = bf16[1,3,512,256]{3,2,1,0:T(8,128)(2,1)S(1)} all-gather(bf16[1,3,32,256]{3,2,1,0:T(8,128)(2,1)S(1)} %get-tuple-element.66), channel_id=2, replica_groups=mesh['dp'=16,'tensor'=2] {'dp'}, dimensions={2}, use_global_device_ids=true | all-gather | bytes 835584 | tf_op jit(solution)/shard_map/all_gather | solution.py:241
  127.7 5.4 copy.116
  163.0 5.6 collective-permute-start
  177.0 6.3 collective-permute-done.2
  186.1 21.7 %collective-permute-done.3 = bf16[1024,256]{0,1:T(8,128)(2,1)S(1)} collective-permute-done((bf16[1024,256]{0,1:T(8,128)(2,1)S(1)}, bf16[1024,256]{0,1:T(8,128)(2,1)S(1)}, u32[]{:S(2)}, u32[]{:S(2)}) %collective-permute-start.3) | collective-permute-done | bytes 524320 | tf_op jit(solution)/shard_map/ppermute | solution.py:248
  208.6 10.4 all-gather.33.cloned.1.call-done
  219.0 12.5 all-gather.19.cloned.1.call-done
  231.5 5.6 multiply_convert_fusion.1
  244.5 9.0 reduce-scatter.19.cloned.1.call-done
  258.0 42.4 %all-gather.4 = bf16[1,256,512]{1,2,0:T(8,128)(2,1)S(1)} all-gather(bf16[1,256,32]{1,2,0:T(8,128)(2,1)S(1)} %get-tuple-element.67), channel_id=6, replica_groups=mesh['dp'=16,'tensor'=2] {'dp'}, dimensions={2}, use_global_device_ids=true | all-gather | bytes 278528 | tf_op jit(solution)/shard_map/all_gather | solution.py:242
  300.4 40.1 %all-gather.3 = bf16[1,3,512,256]{3,2,1,0:T(8,128)(2,1)S(1)} all-gather(bf16[1,3,32,256]{3,2,1,0:T(8,128)(2,1)S(1)} %get-tuple-element.65), channel_id=5, replica_groups=mesh['dp'=16,'tensor'=2] {'dp'}, dimensions={2}, use_global_device_ids=true | all-gather | bytes 835584 | tf_op jit(solution)/shard_map/all_gather | solution.py:241
  371.2 5.0 copy.130
  378.7 5.1 copy.127
  394.4 7.3 copy.132
  413.5 6.5 reduce-scatter.21.cloned.1.call-done
  423.9 5.6 collective-permute-start.4
  437.2 7.0 collective-permute-done.6
  444.4 24.3 %collective-permute-done.7 = bf16[1024,256]{0,1:T(8,128)(2,1)S(1)} collective-permute-done((bf16[1024,256]{0,1:T(8,128)(2,1)S(1)}, bf16[1024,256]{0,1:T(8,128)(2,1)S(1)}, u32[]{:S(2)}, u32[]{:S(2)}) %collective-permute-start.7) | collective-permute-done | bytes 524320 | tf_op jit(solution)/shard_map/ppermute | solution.py:248
  468.7 11.1 all-gather.35.cloned.1.call-done
  479.8 12.7 all-gather.23.cloned.1.call-done
  492.6 6.8 multiply_convert_fusion
  499.4 5.7 all-gather.25.cloned.1.call-done
  505.1 8.1 fusion.148
  517.9 5.4 convolution_convert_fusion.2
  531.0 9.8 reduce-scatter.23.cloned.1.call-done
  547.3 10.4 all-gather.27.cloned.1.call-done
  567.2 5.1 copy.139
  572.4 6.9 multiply_reduce_fusion.1
  604.5 5.1 convert_element_type.366
  625.1 10.2 reduce-scatter.27.cloned.1.call-done
  640.3 11.3 all-gather.29.cloned.1.call-done
  651.6 7.2 fusion.149
  663.6 10.2 reduce-scatter.29.cloned.1.call-done
  685.1 5.9 convolution_convert_fusion.10
  691.1 5.2 fusion.90
  724.4 5.1 copy.153
  729.5 7.4 multiply_reduce_fusion
  757.7 5.2 convert_element_type.385
  800.6 41.6 %reduce-scatter.45.cloned.1.call-done = bf16[1024,32]{0,1:T(8,128)(2,1)} async-done(((bf16[1024,512]{0,1:T(8,128)(2,1)}), bf16[1024,32]{0,1:T(8,128)(2,1)}) %reduce-scatter.45.cloned.1.call-update) | async-done | bytes 65552 | tf_op jit(solution)/shard_map/reduce_scatter | solution.py:214
  843.8 75.7 %reduce-scatter.43.cloned.1.call-done = bf16[32,1024]{1,0:T(8,128)(2,1)} async-done(((bf16[512,1024]{1,0:T(8,128)(2,1)}), bf16[32,1024]{1,0:T(8,128)(2,1)}) %reduce-scatter.43.cloned.1.call-update) | async-done | bytes 65552 | tf_op jit(solution)/shard_map/reduce_scatter | solution.py:211
  919.5 77.2 %reduce-scatter.41.cloned.1.call-done = bf16[32,1024]{1,0:T(8,128)(2,1)} async-done(((bf16[512,1024]{1,0:T(8,128)(2,1)}), bf16[32,1024]{1,0:T(8,128)(2,1)}) %reduce-scatter.41.cloned.1.call-update) | async-done | bytes 65552 | tf_op jit(solution)/shard_map/reduce_scatter | solution.py:211
  1002.5 72.4 %all-reduce.1 = (f32[2,2,256]{2,1,0:T(2,128)}, f32[2,8,169]{2,1,0:T(8,128)}, f32[2,1024]{1,0:T(2,128)}) all-reduce(f32[2,2,256]{2,1,0:T(2,128)S(1)} %pad_maximum_fusion.18, f32[2,8,169]{2,1,0:T(8,128)S(1)} %pad_maximum_fusion.14, f32[2,1024]{1,0:T(2,128)S(1)} %pad_maximum_fusion.15), channel_id=1, replica_groups=mesh['dp'=16,'tensor'=2] {'dp'}, use_global_device_ids=true, to_apply=%region_42.44 | all-reduce | flops 5776 | bytes 46208 | tf_op jit(solution)/shard_map/psum | solution.py:344
  1074.9 73.2 %reduce-scatter.37.cloned.1.call-done = bf16[256,32]{0,1:T(8,128)(2,1)} async-done(((bf16[256,512]{0,1:T(8,128)(2,1)}), bf16[256,32]{0,1:T(8,128)(2,1)}) %reduce-scatter.37.cloned.1.call-update) | async-done | bytes 16400 | tf_op jit(solution)/shard_map/reduce_scatter | solution.py:208
  1149.5 75.4 %reduce-scatter.35.cloned.1.call-done = bf16[3,32,256]{2,1,0:T(8,128)(2,1)} async-done(((bf16[3,512,256]{2,1,0:T(8,128)(2,1)}), bf16[3,32,256]{2,1,0:T(8,128)(2,1)}) %reduce-scatter.35.cloned.1.call-update) | async-done | bytes 49168 | tf_op jit(solution)/shard_map/reduce_scatter | solution.py:205
  1224.9 76.8 %reduce-scatter.33.cloned.1.call-done = bf16[3,32,256]{2,1,0:T(8,128)(2,1)} async-done(((bf16[3,512,256]{2,1,0:T(8,128)(2,1)}), bf16[3,32,256]{2,1,0:T(8,128)(2,1)}) %reduce-scatter.33.cloned.1.call-update) | async-done | bytes 49168 | tf_op jit(solution)/shard_map/reduce_scatter | solution.py:205
  1303.2 6.7 reduce-scatter.31.cloned.1.call-done
  1312.0 41.3 %all-reduce = (f32[2,512]{1,0:T(2,128)}, f32[2,512]{1,0:T(2,128)}, f32[2,512]{1,0:T(2,128)}, f32[2,512]{1,0:T(2,128)}, f32[2,512]{1,0:T(2,128)}, /*index=5*/f32[2,512]{1,0:T(2,128)}) all-reduce(f32[2,512]{1,0:T(2,128)S(1)} %pad_maximum_fusion.16, ...), channel_id=1, replica_groups=mesh['dp'=16,'tensor'=2] {'dp','tensor'}, use_global_device_ids=true, to_apply=%region_32.34 | all-reduce | flops 6144 | bytes 49152 | tf_op jit(solution)/shard_map/psum | solution.py:345
  (525 shorter events, 347.3 us)
Async XLA Ops:
  8.0 90.2 %all-gather.17.cloned.1.call-start = ((), (), s32[]{:S(2)}) async-start(), calls=%async_computation.16 | async-start | bytes 2408448 | tf_op jit(solution)/shard_map/all_gather | solution.py:259
  11.1 244.5 %copy-start.80 = (f32[1,512]{1,0:T(1,128)}, f32[1,512]{1,0:T(1,128)S(1)}, u32[]{:S(2)}) copy-start(f32[1,512]{1,0:T(1,128)S(1)} %get-tuple-element.81) | copy-start | bytes 6148
  13.0 146.4 %reduce-scatter.17.cloned.1.call-start = ((), (), s32[]{:S(2)}) async-start(), calls=%async_computation.17 | async-start | bytes 2408448 | tf_op jit(solution)/shard_map/reduce_scatter | solution.py:293
  14.0 125.2 %copy-start.28 = (f32[8,49,49]{1,2,0:T(8,128)}, f32[8,49,49]{1,2,0:T(8,128)S(1)}, u32[]{:S(2)}) copy-start(f32[8,49,49]{1,2,0:T(8,128)S(1)} %copy.118) | copy-start | bytes 230500
  58.0 91.0 %copy-start.47 = (bf16[1,256,512]{1,2,0:T(8,128)(2,1)}, bf16[1,256,512]{1,2,0:T(8,128)(2,1)S(1)}, u32[]{:S(2)}) copy-start(bf16[1,256,512]{1,2,0:T(8,128)(2,1)S(1)} %all-gather.1) | copy-start | bytes 786436
  152.0 66.9 %all-gather.33.cloned.1.call-start = ((), (), s32[]{:S(2)}) async-start(), calls=%async_computation.40 | async-start | bytes 1114112 | tf_op jit(solution)/shard_map/all_gather | solution.py:243
  152.8 78.7 %all-gather.19.cloned.1.call-start = ((), (), s32[]{:S(2)}) async-start(), calls=%async_computation.18 | async-start | bytes 2408448 | tf_op jit(solution)/shard_map/all_gather | solution.py:303
  162.9 90.6 %reduce-scatter.19.cloned.1.call-start = ((), (), s32[]{:S(2)}) async-start(), calls=%async_computation.19 | async-start | bytes 2408448 | tf_op jit(solution)/shard_map/reduce_scatter | solution.py:308
  163.0 7.5 collective-permute-start
  170.5 5.0 collective-permute-start.1
  175.5 7.7 collective-permute-start.2
  183.3 24.4 %collective-permute-start.3 = (bf16[1024,256]{0,1:T(8,128)(2,1)S(1)}, bf16[1024,256]{0,1:T(8,128)(2,1)S(1)}, u32[]{:S(2)}, u32[]{:S(2)}) collective-permute-start(bf16[1024,256]{0,1:T(8,128)(2,1)S(1)} %pad_maximum_fusion.8), channel_id=1, source_target_pairs={{0,16},{2,18},{4,20},{6,22},{8,24},{10,26},{12,28},{14,30},{16,0},... | collective-permute-start | bytes 1572872 | tf_op jit(solution)/shard_map/ppermute | solution.py:248
  243.3 97.3 %all-gather.21.cloned.1.call-start = ((), (), s32[]{:S(2)}) async-start(), calls=%async_computation.20 | async-start | bytes 2408448 | tf_op jit(solution)/shard_map/all_gather | solution.py:259
  255.2 164.7 %copy-start.5 = (f32[784,512]{1,0:T(8,128)}, f32[784,512]{1,0:T(8,128)S(1)}, u32[]{:S(2)}) copy-start(f32[784,512]{1,0:T(8,128)S(1)} %get-tuple-element.54) | copy-start | bytes 4816900
  256.9 163.1 %reduce-scatter.21.cloned.1.call-start = ((), (), s32[]{:S(2)}) async-start(), calls=%async_computation.21 | async-start | bytes 2408448 | tf_op jit(solution)/shard_map/reduce_scatter | solution.py:293
  300.3 105.5 %copy-start.49 = (bf16[1,256,512]{1,2,0:T(8,128)(2,1)}, bf16[1,256,512]{1,2,0:T(8,128)(2,1)S(1)}, u32[]{:S(2)}) copy-start(bf16[1,256,512]{1,2,0:T(8,128)(2,1)S(1)} %all-gather.4) | copy-start | bytes 786436
  412.7 67.1 %all-gather.35.cloned.1.call-start = ((), (), s32[]{:S(2)}) async-start(), calls=%async_computation.41 | async-start | bytes 1114112 | tf_op jit(solution)/shard_map/all_gather | solution.py:243
  413.4 79.1 %all-gather.23.cloned.1.call-start = ((), (), s32[]{:S(2)}) async-start(), calls=%async_computation.22 | async-start | bytes 2408448 | tf_op jit(solution)/shard_map/all_gather | solution.py:303
  423.9 81.2 %all-gather.25.cloned.1.call-start = ((), (), s32[]{:S(2)}) async-start(), calls=%async_computation.24 | async-start | bytes 2408448 | tf_op jit(solution)/shard_map/all_gather | solution.py:139
  423.9 7.5 collective-permute-start.4
  431.4 5.0 collective-permute-start.5
  432.9 95.4 %reduce-scatter.25.cloned.1.call-start = ((), (), s32[]{:S(2)}) async-start(), calls=%async_computation.25 | async-start | bytes 2408448 | tf_op jit(solution)/shard_map/reduce_scatter | solution.py:147
  436.5 7.7 collective-permute-start.6
  444.2 24.4 %collective-permute-start.7 = (bf16[1024,256]{0,1:T(8,128)(2,1)S(1)}, bf16[1024,256]{0,1:T(8,128)(2,1)S(1)}, u32[]{:S(2)}, u32[]{:S(2)}) collective-permute-start(bf16[1024,256]{0,1:T(8,128)(2,1)S(1)} %pad_maximum_fusion.9), channel_id=1, source_target_pairs={{0,16},{2,18},{4,20},{6,22},{8,24},{10,26},{12,28},{14,30},{16,0},... | collective-permute-start | bytes 1572872 | tf_op jit(solution)/shard_map/ppermute | solution.py:248
  517.8 23.0 %reduce-scatter.23.cloned.1.call-start = ((), (), s32[]{:S(2)}) async-start(), calls=%async_computation.23 | async-start | bytes 2408448 | tf_op jit(solution)/shard_map/reduce_scatter | solution.py:308
  523.3 34.4 %all-gather.27.cloned.1.call-start = ((), (), s32[]{:S(2)}) async-start(), calls=%async_computation.26 | async-start | bytes 2408448 | tf_op jit(solution)/shard_map/all_gather | solution.py:156
  546.6 88.7 %reduce-scatter.27.cloned.1.call-start = ((), (), s32[]{:S(2)}) async-start(), calls=%async_computation.27 | async-start | bytes 2408448 | tf_op jit(solution)/shard_map/reduce_scatter | solution.py:196
  625.0 26.6 %all-gather.29.cloned.1.call-start = ((), (), s32[]{:S(2)}) async-start(), calls=%async_computation.28 | async-start | bytes 2408448 | tf_op jit(solution)/shard_map/all_gather | solution.py:139
  640.3 33.5 %reduce-scatter.29.cloned.1.call-start = ((), (), s32[]{:S(2)}) async-start(), calls=%async_computation.29 | async-start | bytes 2408448 | tf_op jit(solution)/shard_map/reduce_scatter | solution.py:147
  663.6 50.8 %all-gather.31.cloned.1.call-start = ((), (), s32[]{:S(2)}) async-start(), calls=%async_computation.30 | async-start | bytes 2408448 | tf_op jit(solution)/shard_map/all_gather | solution.py:156
  679.4 121.3 %reduce-scatter.47.cloned.1.call-start = ((), (), s32[]{:S(2)}) async-start(), calls=%async_computation.39 | async-start | bytes 1114112 | tf_op jit(solution)/shard_map/reduce_scatter | solution.py:214
  685.1 157.1 %reduce-scatter.45.cloned.1.call-start = ((), (), s32[]{:S(2)}) async-start(), calls=%async_computation.38 | async-start | bytes 1114112 | tf_op jit(solution)/shard_map/reduce_scatter | solution.py:214
  691.0 228.5 %reduce-scatter.43.cloned.1.call-start = ((), (), s32[]{:S(2)}) async-start(), calls=%async_computation.37 | async-start | bytes 1114112 | tf_op jit(solution)/shard_map/reduce_scatter | solution.py:211
  696.3 300.4 %reduce-scatter.41.cloned.1.call-start = ((), (), s32[]{:S(2)}) async-start(), calls=%async_computation.36 | async-start | bytes 1114112 | tf_op jit(solution)/shard_map/reduce_scatter | solution.py:211
  701.6 373.3 %reduce-scatter.39.cloned.1.call-start = ((), (), s32[]{:S(2)}) async-start(), calls=%async_computation.35 | async-start | bytes 278528 | tf_op jit(solution)/shard_map/reduce_scatter | solution.py:208
  712.9 435.3 %reduce-scatter.37.cloned.1.call-start = ((), (), s32[]{:S(2)}) async-start(), calls=%async_computation.34 | async-start | bytes 278528 | tf_op jit(solution)/shard_map/reduce_scatter | solution.py:208
  717.4 507.5 %reduce-scatter.35.cloned.1.call-start = ((), (), s32[]{:S(2)}) async-start(), calls=%async_computation.33 | async-start | bytes 835584 | tf_op jit(solution)/shard_map/reduce_scatter | solution.py:205
  720.5 581.2 %reduce-scatter.33.cloned.1.call-start = ((), (), s32[]{:S(2)}) async-start(), calls=%async_computation.32 | async-start | bytes 835584 | tf_op jit(solution)/shard_map/reduce_scatter | solution.py:205
  780.0 529.9 %reduce-scatter.31.cloned.1.call-start = ((), (), s32[]{:S(2)}) async-start(), calls=%async_computation.31 | async-start | bytes 2408448 | tf_op jit(solution)/shard_map/reduce_scatter | solution.py:196
  799.4 198.9 %copy-start.100 = (f32[512]{0:T(512)S(1)}, f32[512]{0:T(512)}, u32[]{:S(2)}) copy-start(f32[512]{0:T(512)} %get-tuple-element.18) | copy-start | bytes 6148
  799.4 198.9 %copy-start.99 = (f32[512]{0:T(512)S(1)}, f32[512]{0:T(512)}, u32[]{:S(2)}) copy-start(f32[512]{0:T(512)} %get-tuple-element.29) | copy-start | bytes 6148
  799.4 198.9 %copy-start.87 = (f32[512]{0:T(512)S(1)}, f32[512]{0:T(512)}, u32[]{:S(2)}) copy-start(f32[512]{0:T(512)} %get-tuple-element.49) | copy-start | bytes 6148
  799.4 198.9 %copy-start.57 = (f32[8,49,49]{1,2,0:T(8,128)S(1)}, f32[8,49,49]{1,2,0:T(8,128)}, u32[]{:S(2)}) copy-start(f32[8,49,49]{1,2,0:T(8,128)} %get-tuple-element.41) | copy-start | bytes 230500
  998.6 311.3 %copy-start.67 = (f32[784]{0:T(1024)S(1)}, f32[784]{0:T(1024)}, u32[]{:S(2)}) copy-start(f32[784]{0:T(1024)} %copy-done.66) | copy-start | bytes 9412
  998.6 311.3 %copy-start.74 = (f32[784]{0:T(1024)S(1)}, f32[784]{0:T(1024)}, u32[]{:S(2)}) copy-start(f32[784]{0:T(1024)} %copy-done.73) | copy-start | bytes 9412
  998.6 311.3 %copy-start.78 = (f32[1,512]{1,0:T(1,128)S(1)}, f32[1,512]{1,0:T(1,128)}, u32[]{:S(2)}) copy-start(f32[1,512]{1,0:T(1,128)} %copy-done.77) | copy-start | bytes 6148
  1001.3 308.6 %copy-start.4 = (bf16[784,512]{1,0:T(8,128)(2,1)S(1)}, bf16[784,512]{1,0:T(8,128)(2,1)}, u32[]{:S(2)}) copy-start(bf16[784,512]{1,0:T(8,128)(2,1)} %param.19) | copy-start | bytes 2408452
  1001.3 352.0 %copy-start.20 = (f32[784,512]{1,0:T(8,128)S(1)}, f32[784,512]{1,0:T(8,128)}, u32[]{:S(2)}) copy-start(f32[784,512]{1,0:T(8,128)} %copy-done.19) | copy-start | bytes 4816900
  (110 other events, 759.5 us)
Sparse Core Ops, SparseCore 0:
  13.1 12.5 all-gather.16
  152.1 7.1 reduce-scatter.16
  257.0 11.1 all-gather.20
  412.8 7.1 reduce-scatter.20
  518.0 10.3 reduce-scatter.24
  530.4 10.3 reduce-scatter.22
  640.4 11.1 all-gather.28
  679.5 11.1 all-gather.30
Sparse Core Ops, SparseCore 1:
  155.8 63.1 all-gather.32
  221.0 10.5 all-gather.18
  243.4 10.1 reduce-scatter.18
  416.8 62.9 all-gather.34
  481.9 10.5 all-gather.22
  494.1 10.9 all-gather.24
  546.7 11.0 all-gather.26
  625.1 10.1 reduce-scatter.26
  663.6 10.1 reduce-scatter.28
  685.2 79.9 reduce-scatter.46
  767.2 75.0 reduce-scatter.44
  844.5 74.9 reduce-scatter.42
  921.6 75.0 reduce-scatter.40
  999.0 73.3 reduce-scatter.38
  1074.6 73.5 reduce-scatter.36
  1150.4 74.4 reduce-scatter.34
  1227.2 74.5 reduce-scatter.32
  1304.6 5.3 reduce-scatter.30
